TPU v7x, 256 devices: a whole 4x4x8 slice. The times are simulated.
256 devices in a mesh: dp: 16 (over z, core), mp: 16 (over y, x).
Axes of the slice: x: 4, y: 4, z: 8, core: 2. Of those that a mesh axis runs over, the one named last changes fastest.
Arguments:
- candidates: bfloat16 [4096, 4096], P('dp', 'mp'), may hold values from -6 to 6
- hold_gate: bfloat16 [4096, 8192], P(None, 'mp'), may hold values from -0.09375 to 0.09375
- hold_up: bfloat16 [4096, 8192], P(None, 'mp'), may hold values from -0.09375 to 0.09375
- probe: float32 [8192], P('mp'), as said below
- chosen: int32 [16, 192], replicated, may hold values from 0 to 4095, as said below
- counts: int32 [16], replicated, may hold values from 24 to 192, as said below
- gate_w: bfloat16 [4096, 14336], P('dp', 'mp'), may hold values from -0.09375 to 0.09375
- up_w: bfloat16 [4096, 14336], P('dp', 'mp'), may hold values from -0.09375 to 0.09375
- cotangent: bfloat16 [3072, 14336], P('dp', 'mp'), may hold values from -6 to 6
Outputs:
- grad_gate: bfloat16 [4096, 14336], P('dp', 'mp')
- grad_up: bfloat16 [4096, 14336], P('dp', 'mp')
- hidden: bfloat16 [3072, 14336], P('dp', 'mp')
- cand_weight: float32 [4096], P('dp')
Inputs may be any that keep to these rules, and one draw needn't show every extreme that they name: `chosen`: all entries are distinct candidate indices. `counts`: exactly one training shard uses all 192 slots in every draw. `probe`: magnitudes at most 12 / sqrt(8192).
All inputs are finite; a program needn't handle non-finite values.
Results may differ from a plain program's by a relative error of at most 0.0057.
Values may be sent and summed in bfloat16 or wider, within the bound.
A program may use at most 128 MiB of HBM per device.

v0:
```python
import jax
import jax.numpy as jnp
from jax import lax
from jax.sharding import PartitionSpec as P


def gather_by_a2a(x, axis_name, axis):
    parts = lax.psum(1, axis_name)
    stacked = lax.all_to_all(
        jnp.broadcast_to(x[None], (parts,) + x.shape),
        axis_name,
        split_axis=0,
        concat_axis=0,
        tiled=True,
    )
    stacked = jnp.moveaxis(stacked, 0, axis)
    shape = list(x.shape)
    shape[axis] *= parts
    return stacked.reshape(shape)


def gather_rows(x):
    by_z = lax.all_gather(x, "z", axis=0)
    both = lax.all_gather(by_z, "core", axis=1)
    return both.reshape((-1,) + x.shape[1:])


def on_device(candidates, hold_gate, hold_up, probe, chosen, counts, gate_w, up_w, cotangent):
    cand_dev = candidates.shape[0]
    shards = chosen.shape[0]
    slots = chosen.shape[1]
    full_w = (gather_rows(gate_w), gather_rows(up_w))
    own_index = lax.axis_index("z") * lax.psum(1, "core") + lax.axis_index("core")
    source = chosen // cand_dev
    local_row = (chosen % cand_dev).reshape(-1)
    usable = (
        (jnp.arange(slots, dtype=jnp.int32)[None, :] < counts[:, None]) & (source == own_index)
    ).reshape(-1)
    onehot = (
        (local_row[:, None] == jnp.arange(cand_dev, dtype=jnp.int32)[None, :]) & usable[:, None]
    ).astype(jnp.bfloat16)
    picked = jnp.dot(onehot, candidates, preferred_element_type=jnp.float32).astype(jnp.bfloat16)
    picked = picked.reshape(shards, slots, candidates.shape[1])
    arrived = lax.all_to_all(picked, DP, split_axis=0, concat_axis=0, tiled=True)
    row_slab = jnp.sum(arrived.astype(jnp.float32), axis=0).astype(jnp.bfloat16)
    row_x = gather_by_a2a(row_slab, "mp", 1)
    row_slices = lax.all_to_all(row_x, DP, split_axis=1, concat_axis=0, tiled=True)
    incoming = gather_by_a2a(candidates, "mp", 1)
    hold_g = jnp.dot(incoming, hold_gate, preferred_element_type=jnp.float32)
    hold_u = jnp.dot(incoming, hold_up, preferred_element_type=jnp.float32)
    partial_score = jnp.sum(jax.nn.silu(hold_g) * hold_u * probe[None, :], axis=1)
    score = lax.psum(partial_score, "mp")
    cand_weight = jax.nn.sigmoid(score)
    picked_weight = (
        jnp.dot(
            onehot, cand_weight.astype(jnp.bfloat16)[:, None], preferred_element_type=jnp.float32
        )
        .astype(jnp.bfloat16)
        .reshape(shards, slots)
    )
    arrived_weight = lax.all_to_all(picked_weight, DP, split_axis=0, concat_axis=0, tiled=True)
    row_weight = jnp.sum(arrived_weight.astype(jnp.float32), axis=0)
    gate = jnp.dot(row_x, full_w[0], preferred_element_type=jnp.float32)
    up = jnp.dot(row_x, full_w[1], preferred_element_type=jnp.float32)
    hidden = (jax.nn.silu(gate) * up).astype(jnp.bfloat16)
    back = cotangent.astype(jnp.float32) * row_weight[:, None]
    sig = jax.nn.sigmoid(gate)
    d_up = (back * gate * sig).astype(jnp.bfloat16)
    d_gate = (back * up * sig * (1.0 + gate * (1.0 - sig))).astype(jnp.bfloat16)
    contract_rows = (((0,), (0,)), ((), ()))
    incoming = (gather_rows(d_gate), gather_rows(d_up))
    grad_g = lax.dot_general(
        row_slices, incoming[0], contract_rows, preferred_element_type=jnp.float32
    )
    grad_u = lax.dot_general(
        row_slices, incoming[1], contract_rows, preferred_element_type=jnp.float32
    )
    return (grad_g.astype(jnp.bfloat16), grad_u.astype(jnp.bfloat16), hidden, cand_weight)


DP = ("z", "core")


def solution(mesh):
    cores = 2
    mesh = jax.sharding.Mesh(
        mesh.devices.reshape(mesh.devices.shape[0] // cores, cores, mesh.devices.shape[1]),
        ("z", "core", "mp"),
    )
    placed = (
        P(DP, "mp"),
        P(None, "mp"),
        P(None, "mp"),
        P("mp"),
        P(),
        P(),
        P(DP, "mp"),
        P(DP, "mp"),
        P(DP, "mp"),
    )
    return jax.shard_map(
        on_device,
        mesh=mesh,
        in_specs=placed,
        out_specs=(P(DP, "mp"), P(DP, "mp"), P(DP, "mp"), P(DP)),
        check_vma=False,
    )
```

profile of v0, /device:TPU:1, one launch (start us, length us, event | category | flops | bytes accessed | tf_op | source)
XLA Modules:
  0.0 406.3 jit_solution(17809317110289626407)
XLA Ops:
  8.7 54.6 %all-gather.21.cloned.1.call-done = bf16[2048,896]{1,0:T(8,128)(2,1)} async-done(((bf16[256,896]{1,0:T(8,128)(2,1)}), bf16[2048,896]{1,0:T(8,128)(2,1)}) %all-gather.21.cloned.1.call-update) | async-done | bytes 3670032 | tf_op jit(solution)/shard_map/all_gather | solution.py:23
  63.3 50.2 %all-gather.17.cloned.1.call-done = bf16[2048,896]{1,0:T(8,128)(2,1)} async-done(((bf16[256,896]{1,0:T(8,128)(2,1)}), bf16[2048,896]{1,0:T(8,128)(2,1)}) %all-gather.17.cloned.1.call-update) | async-done | bytes 3670032 | tf_op jit(solution)/shard_map/all_gather | solution.py:23
  113.7 1.5 broadcast_in_dim.5
  115.2 6.5 %all-to-all-start.3 = ((bf16[16,256,256]{1,2,0:T(8,128)(2,1)}), bf16[16,256,256]{1,2,0:T(8,128)(2,1)S(1)}, u32[]{:S(2)}, u32[]{:S(2)}) async-start(bf16[16,256,256]{1,2,0:T(8,128)(2,1)} %broadcast_in_dim.5), calls=%async_computation.3 | async-start | bytes 4194304 | tf_op jit(solution)/shard_map/all_to_all | solution.py:9
  122.0 3.5 convolution_convert_fusion
  125.5 26.5 %all-to-all-done.3 = bf16[16,256,256]{1,2,0:T(8,128)(2,1)S(1)} async-done(((bf16[16,256,256]{1,2,0:T(8,128)(2,1)}), bf16[16,256,256]{1,2,0:T(8,128)(2,1)S(1)}, u32[]{:S(2)}, u32[]{:S(2)}) %all-to-all-start.3) | async-done | bytes 2097184 | tf_op jit(solution)/shard_map/all_to_all | solution.py:9
  152.0 1.3 copy-done
  153.3 6.6 %all-to-all-start = ((bf16[16,192,256]{2,1,0:T(8,128)(2,1)}), bf16[16,192,256]{2,1,0:T(8,128)(2,1)S(1)}, u32[]{:S(2)}, u32[]{:S(2)}) async-start(bf16[16,192,256]{2,1,0:T(8,128)(2,1)} %bitcast.41), calls=%async_computation | async-start | bytes 3145728 | tf_op jit(solution)/shard_map/all_to_all | solution.py:44
  159.9 4.3 %fusion.15 = f32[256,512]{1,0:T(8,128)S(1)} fusion(bf16[256,4096]{0,1:T(8,128)(2,1)} %bitcast.39, bf16[4096,512]{1,0:T(8,128)(2,1)} %param.10), kind=kOutput, calls=%fused_computation.32 | convolution fusion | flops 1073741824 | bytes 6815744 | tf_op jit(solution)/shard_map/dot_general | solution.py:49
  164.6 1.4 fusion.9
  166.0 31.8 %psum.7 = f32[256]{0:T(256)S(1)} all-reduce(f32[256]{0:T(256)S(1)} %fusion.9), channel_id=1, replica_groups=mesh['z'=8,'core'=2,'mp'=16] {'mp'}, use_global_device_ids=true, to_apply=%region_2.3 | all-reduce | flops 256 | bytes 2048 | tf_op jit(solution)/shard_map/psum | solution.py:52
  198.4 2.5 fusion.1
  201.6 13.7 %all-to-all-start.4 = ((bf16[16,1,192]{2,1,0:T(2,128)(2,1)}), bf16[16,1,192]{2,1,0:T(2,128)(2,1)S(1)}, u32[]{:S(2)}, u32[]{:S(2)}) async-start(bf16[16,1,192]{2,1,0:T(2,128)(2,1)} %all_to_all.35), calls=%async_computation.4 | async-start | bytes 32768 | tf_op jit(solution)/shard_map/all_to_all | solution.py:61
  215.6 7.1 %all-to-all-done.4 = bf16[16,1,192]{2,1,0:T(2,128)(2,1)S(1)} async-done(((bf16[16,1,192]{2,1,0:T(2,128)(2,1)}), bf16[16,1,192]{2,1,0:T(2,128)(2,1)S(1)}, u32[]{:S(2)}, u32[]{:S(2)}) %all-to-all-start.4) | async-done | bytes 6176 | tf_op jit(solution)/shard_map/all_to_all | solution.py:61
  222.7 1.3 broadcast_in_dim.4
  224.0 3.7 all-to-all-start.1
  227.8 24.8 %all-to-all-done.1 = bf16[16,192,256]{2,1,0:T(8,128)(2,1)S(1)} async-done(((bf16[16,192,256]{2,1,0:T(8,128)(2,1)}), bf16[16,192,256]{2,1,0:T(8,128)(2,1)S(1)}, u32[]{:S(2)}, u32[]{:S(2)}) %all-to-all-start.1) | async-done | bytes 1572896 | tf_op jit(solution)/shard_map/all_to_all | solution.py:9
  252.9 5.8 %fusion.16 = f32[192,896]{1,0:T(8,128)} fusion(bf16[192,4096]{1,0:T(8,128)(2,1)S(1)} %bitcast.42, bf16[4096,896]{1,0:T(8,128)(2,1)} %bitcast.47), kind=kOutput, calls=%fused_computation.33 | convolution fusion | flops 1409286144 | bytes 9601024 | tf_op jit(solution)/shard_map/dot_general | solution.py:63
  258.7 6.1 %multiply_convert_fusion = (bf16[192,896]{1,0:T(8,128)(2,1)}, bf16[192,896]{1,0:T(8,128)(2,1)}, bf16[192,896]{1,0:T(8,128)(2,1)}) fusion(f32[192,896]{1,0:T(8,128)} %fusion.16, f32[192]{0:T(256)S(1)} %convert_reduce_fusion, bf16[192,896]{1,0:T(8,128)(2,1)S(1)} %copy-done.6, bf16[192,4096]{1,0:T(8,128)(2,1)S(1)} %bitcast.43, bf16[4096,896]{1,0:T(8,128)(2,1)} %bitcast.48), kind=kOutput, calls=%fused_computation.13 | convolution fusion | flops 1412382720 | bytes 10978048 | tf_op jit(solution)/shard_map/dot_general | solution.py:64
  265.5 32.7 %all-gather.29.cloned.1.call-done = bf16[1536,896]{1,0:T(8,128)(2,1)} async-done(((bf16[192,896]{1,0:T(8,128)(2,1)}), bf16[1536,896]{1,0:T(8,128)(2,1)}) %all-gather.29.cloned.1.call-update) | async-done | bytes 2752528 | tf_op jit(solution)/shard_map/all_gather | solution.py:23
  298.3 43.6 %all-gather.25.cloned.1.call-done = bf16[1536,896]{1,0:T(8,128)(2,1)} async-done(((bf16[192,896]{1,0:T(8,128)(2,1)}), bf16[1536,896]{1,0:T(8,128)(2,1)}) %all-gather.25.cloned.1.call-update) | async-done | bytes 2752528 | tf_op jit(solution)/shard_map/all_gather | solution.py:23
  341.9 47.2 %all_to_all.41 = bf16[192,16,256]{2,0,1:T(8,128)(2,1)S(1)} all-to-all(bf16[192,16,256]{2,0,1:T(8,128)(2,1)S(1)} %bitcast.34), channel_id=1, replica_groups=mesh['z'=8,'core'=2,'mp'=16] {'z','core'}, dimensions={1} | all-to-all | bytes 3145728 | tf_op jit(solution)/shard_map/all_to_all | solution.py:47
  389.1 5.2 %convolution_convert_fusion.1 = bf16[256,896]{1,0:T(8,128)(2,1)} fusion(bf16[3072,256]{1,0:T(8,128)(2,1)S(1)} %bitcast.44, bf16[3072,896]{1,0:T(8,128)(2,1)} %bitcast.49), kind=kOutput, calls=%fused_computation.8 | convolution fusion | flops 1409515520 | bytes 7536640 | tf_op jit(solution)/shard_map/dot_general | solution.py:75
  394.3 5.2 %convolution_convert_fusion.2 = bf16[256,896]{1,0:T(8,128)(2,1)} fusion(bf16[3072,256]{1,0:T(8,128)(2,1)S(1)} %bitcast.45, bf16[3072,896]{1,0:T(8,128)(2,1)} %bitcast.50), kind=kOutput, calls=%fused_computation.9 | convolution fusion | flops 1409515520 | bytes 7536640 | tf_op jit(solution)/shard_map/dot_general | solution.py:72
  (48 shorter events, 4.9 us)
Async XLA Ops:
  7.2 56.1 %all-gather.21.cloned.1.call-start = ((), (), s32[]{:S(2)}) async-start(), calls=%async_computation.7 | async-start | bytes 4128768 | tf_op jit(solution)/shard_map/all_gather | solution.py:23
  7.9 105.6 %all-gather.17.cloned.1.call-start = ((), (), s32[]{:S(2)}) async-start(), calls=%async_computation.5 | async-start | bytes 4128768 | tf_op jit(solution)/shard_map/all_gather | solution.py:23
  8.6 244.2 %all-gather.23.cloned.1.call-start = ((), (), s32[]{:S(2)}) async-start(), calls=%async_computation.8 | async-start | bytes 11010048 | tf_op jit(solution)/shard_map/all_gather | solution.py:24
  63.3 50.3 %copy-start.2 = (bf16[256,256]{1,0:T(8,128)(2,1)S(1)}, bf16[256,256]{1,0:T(8,128)(2,1)}, u32[]{:S(2)}) copy-start(bf16[256,256]{1,0:T(8,128)(2,1)} %param.9) | copy-start | bytes 393220
  63.3 195.5 %all-gather.19.cloned.1.call-start = ((), (), s32[]{:S(2)}) async-start(), calls=%async_computation.6 | async-start | bytes 11010048 | tf_op jit(solution)/shard_map/all_gather | solution.py:24
  113.6 8.1 %copy-start.3 = (s32[16,192]{1,0:T(8,128)S(1)}, s32[16,192]{1,0:T(8,128)}, u32[]{:S(2)}) copy-start(s32[16,192]{1,0:T(8,128)} %param.13) | copy-start | bytes 36868
  113.7 8.1 %copy-start.4 = (s32[16]{0:T(128)S(1)}, s32[16]{0:T(128)}, u32[]{:S(2)}) copy-start(s32[16]{0:T(128)} %param.14) | copy-start | bytes 196
  115.2 36.8 %all-to-all-start.3 = ((bf16[16,256,256]{1,2,0:T(8,128)(2,1)}), bf16[16,256,256]{1,2,0:T(8,128)(2,1)S(1)}, u32[]{:S(2)}, u32[]{:S(2)}) async-start(bf16[16,256,256]{1,2,0:T(8,128)(2,1)} %broadcast_in_dim.5), calls=%async_computation.3 | async-start | bytes 4194304 | tf_op jit(solution)/shard_map/all_to_all | solution.py:9
  152.0 1.3 copy-start
  153.3 48.3 %all-to-all-start = ((bf16[16,192,256]{2,1,0:T(8,128)(2,1)}), bf16[16,192,256]{2,1,0:T(8,128)(2,1)S(1)}, u32[]{:S(2)}, u32[]{:S(2)}) async-start(bf16[16,192,256]{2,1,0:T(8,128)(2,1)} %bitcast.41), calls=%async_computation | async-start | bytes 3145728 | tf_op jit(solution)/shard_map/all_to_all | solution.py:44
  159.9 4.3 %copy-start.1 = (bf16[16,256,256]{1,2,0:T(8,128)(2,1)S(1)}, bf16[16,256,256]{1,2,0:T(8,128)(2,1)}, u32[]{:S(2)}) copy-start(bf16[16,256,256]{1,2,0:T(8,128)(2,1)} %copy-done) | copy-start | bytes 6291460
  159.9 4.8 %copy-start.5 = (bf16[4096,512]{1,0:T(8,128)(2,1)S(1)}, bf16[4096,512]{1,0:T(8,128)(2,1)}, u32[]{:S(2)}) copy-start(bf16[4096,512]{1,0:T(8,128)(2,1)} %param.11) | copy-start | bytes 12582916
  159.9 4.8 %copy-start.7 = (f32[512]{0:T(512)S(1)}, f32[512]{0:T(512)}, u32[]{:S(2)}) copy-start(f32[512]{0:T(512)} %param.12) | copy-start | bytes 6148
  201.6 21.1 %all-to-all-start.4 = ((bf16[16,1,192]{2,1,0:T(2,128)(2,1)}), bf16[16,1,192]{2,1,0:T(2,128)(2,1)S(1)}, u32[]{:S(2)}, u32[]{:S(2)}) async-start(bf16[16,1,192]{2,1,0:T(2,128)(2,1)} %all_to_all.35), calls=%async_computation.4 | async-start | bytes 32768 | tf_op jit(solution)/shard_map/all_to_all | solution.py:61
  224.0 28.6 %all-to-all-start.1 = ((bf16[16,192,256]{2,1,0:T(8,128)(2,1)}), bf16[16,192,256]{2,1,0:T(8,128)(2,1)S(1)}, u32[]{:S(2)}, u32[]{:S(2)}) async-start(bf16[16,192,256]{2,1,0:T(8,128)(2,1)} %broadcast_in_dim.4), calls=%async_computation.1 | async-start | bytes 3145728 | tf_op jit(solution)/shard_map/all_to_all | solution.py:9
  227.8 70.5 %all-gather.29.cloned.1.call-start = ((), (), s32[]{:S(2)}) async-start(), calls=%async_computation.11 | async-start | bytes 3096576 | tf_op jit(solution)/shard_map/all_gather | solution.py:23
  252.9 5.9 %copy-start.6 = (bf16[192,896]{1,0:T(8,128)(2,1)S(1)}, bf16[192,896]{1,0:T(8,128)(2,1)}, u32[]{:S(2)}) copy-start(bf16[192,896]{1,0:T(8,128)(2,1)} %param.17) | copy-start | bytes 1032196
  264.9 77.0 %all-gather.25.cloned.1.call-start = ((), (), s32[]{:S(2)}) async-start(), calls=%async_computation.9 | async-start | bytes 3096576 | tf_op jit(solution)/shard_map/all_gather | solution.py:23
  265.5 123.6 %all-gather.31.cloned.1.call-start = ((), (), s32[]{:S(2)}) async-start(), calls=%async_computation.12 | async-start | bytes 8257536 | tf_op jit(solution)/shard_map/all_gather | solution.py:24
  298.3 96.0 %all-gather.27.cloned.1.call-start = ((), (), s32[]{:S(2)}) async-start(), calls=%async_computation.10 | async-start | bytes 8257536 | tf_op jit(solution)/shard_map/all_gather | solution.py:24
Sparse Core Ops, SparseCore 0:
  9.8 53.4 all-gather.20
  65.0 48.4 all-gather.16
  115.3 23.1 all-gather.22
  140.1 25.0 all-gather.18
  265.0 33.1 all-gather.28
  300.4 41.3 all-gather.24
  343.6 23.0 all-gather.30
  368.5 22.2 all-gather.26
where the time goes:
time: 407 us; the launch traced here: 406 us
  waiting for transfers between devices  241 us (59%)
  blocking collectives  79.1 us (19%)
  matrix products  33.9 us (8%)
  starting transfers between devices  30.9 us (8%)
  between operations  14.3 us (4%)
  local copies, waits for them, and re-layouts  5.83 us (1%)
    all_gather x4, waiting for transfers between devices, gather_rows(): by_z = lax.all_gather(x, 'z', axis=0)  181 us
    all_to_all x2, waiting for transfers between devices, gather_by_a2a(): lax.all_to_all(jnp.broadcast_to(x[None], (parts,) + x.shape), axis_name,...  51.3 us
    all_to_all x1, blocking collectives, on_device(): lax.all_to_all(row_x, DP, split_axis=1, concat_axis=0, tiled=True)  47.2 us
    psum x1, blocking collectives, on_device(): score = lax.psum(partial_score, 'mp')  31.8 us
    all_to_all x1, starting transfers between devices, on_device(): lax.all_to_all(picked_weight, DP, split_axis=0, concat_axis=0, tiled=True)  13.7 us
    all_to_all x2, starting transfers between devices, gather_by_a2a(): lax.all_to_all(jnp.broadcast_to(x[None], (parts,) + x.shape), axis_name,...  10.2 us
  transfers between devices with their start and end apart: 12, of which 7 were waited for; matrix products, arithmetic and copies ran while one was open for 7% of the time, Pallas kernels for 0%

commit v1 on v0

--- a/solution.py
+++ b/solution.py
@@ -2,6 +2,16 @@
 import jax.numpy as jnp
 from jax import lax
 from jax.sharding import PartitionSpec as P
+
+touch_rails_in = lambda x0: jnp.concatenate(
+    jax.lax.all_to_all(
+        jnp.stack(jnp.split(x0, jax.lax.axis_size(DP), 1)),
+        axis_name=DP,
+        split_axis=0,
+        concat_axis=0,
+    ),
+    0,
+)
 
 
 def gather_by_a2a(x, axis_name, axis):
@@ -44,7 +54,7 @@
     arrived = lax.all_to_all(picked, DP, split_axis=0, concat_axis=0, tiled=True)
     row_slab = jnp.sum(arrived.astype(jnp.float32), axis=0).astype(jnp.bfloat16)
     row_x = gather_by_a2a(row_slab, "mp", 1)
-    row_slices = lax.all_to_all(row_x, DP, split_axis=1, concat_axis=0, tiled=True)
+    row_slices = touch_rails_in(row_x)
     incoming = gather_by_a2a(candidates, "mp", 1)
     hold_g = jnp.dot(incoming, hold_gate, preferred_element_type=jnp.float32)
     hold_u = jnp.dot(incoming, hold_up, preferred_element_type=jnp.float32)

time: 407 us -> 407 us (level)
  transfers between devices with their start and end apart: 12 -> 12, of which waited for: 7 -> 7; matrix products, arithmetic and copies ran while one was open for 7% -> 6% of each run, Pallas kernels for 0% -> 0%
where the time goes in v1:
time: 407 us; the launch traced here: 406 us
  waiting for transfers between devices  241 us (59%)
  blocking collectives  78.7 us (19%)
  matrix products  32.8 us (8%)
  starting transfers between devices  31.1 us (8%)
  between operations  14.4 us (4%)
  local copies, waits for them, and re-layouts  6.86 us (2%)
    all_gather x4, waiting for transfers between devices, gather_rows(): by_z = lax.all_gather(x, 'z', axis=0)  181 us
    all_to_all x2, waiting for transfers between devices, gather_by_a2a(): lax.all_to_all(jnp.broadcast_to(x[None], (parts,) + x.shape), axis_name,...  51.3 us
    all_to_all x1, blocking collectives, jax.lax.all_to_all(jnp.stack(jnp.split(x0, jax.lax.axis_size(DP), 1)), ax...  47.2 us
    psum x1, blocking collectives, on_device(): score = lax.psum(partial_score, 'mp')  31.5 us
    all_to_all x1, starting transfers between devices, on_device(): lax.all_to_all(picked_weight, DP, split_axis=0, concat_axis=0, tiled=True)  13.8 us
    all_to_all x2, starting transfers between devices, gather_by_a2a(): lax.all_to_all(jnp.broadcast_to(x[None], (parts,) + x.shape), axis_name,...  10.4 us
  transfers between devices with their start and end apart: 12, of which 7 were waited for; matrix products, arithmetic and copies ran while one was open for 6% of the time, Pallas kernels for 0%

profile of v1, /device:TPU:1, one launch (start us, length us, event | category | flops | bytes accessed | tf_op | source)
XLA Modules:
  0.0 406.1 jit_solution(143910329578058968)
XLA Ops:
  8.7 54.6 %all-gather.21.cloned.1.call-done = bf16[2048,896]{1,0:T(8,128)(2,1)} async-done(((bf16[256,896]{1,0:T(8,128)(2,1)}), bf16[2048,896]{1,0:T(8,128)(2,1)}) %all-gather.21.cloned.1.call-update) | async-done | bytes 3670032 | tf_op jit(solution)/shard_map/all_gather | solution.py:33
  63.3 50.2 %all-gather.17.cloned.1.call-done = bf16[2048,896]{1,0:T(8,128)(2,1)} async-done(((bf16[256,896]{1,0:T(8,128)(2,1)}), bf16[2048,896]{1,0:T(8,128)(2,1)}) %all-gather.17.cloned.1.call-update) | async-done | bytes 3670032 | tf_op jit(solution)/shard_map/all_gather | solution.py:33
  114.5 1.5 broadcast_in_dim.5
  116.0 6.7 %all-to-all-start.3 = ((bf16[16,256,256]{1,2,0:T(8,128)(2,1)}), bf16[16,256,256]{1,2,0:T(8,128)(2,1)S(1)}, u32[]{:S(2)}, u32[]{:S(2)}) async-start(bf16[16,256,256]{1,2,0:T(8,128)(2,1)} %broadcast_in_dim.5), calls=%async_computation.3 | async-start | bytes 4194304 | tf_op jit(solution)/shard_map/all_to_all | solution.py:19
  123.0 3.5 convolution_convert_fusion
  126.5 26.5 %all-to-all-done.3 = bf16[16,256,256]{1,2,0:T(8,128)(2,1)S(1)} async-done(((bf16[16,256,256]{1,2,0:T(8,128)(2,1)}), bf16[16,256,256]{1,2,0:T(8,128)(2,1)S(1)}, u32[]{:S(2)}, u32[]{:S(2)}) %all-to-all-start.3) | async-done | bytes 2097184 | tf_op jit(solution)/shard_map/all_to_all | solution.py:19
  152.9 1.3 copy-done
  154.3 6.6 %all-to-all-start = ((bf16[16,192,256]{2,1,0:T(8,128)(2,1)}), bf16[16,192,256]{2,1,0:T(8,128)(2,1)S(1)}, u32[]{:S(2)}, u32[]{:S(2)}) async-start(bf16[16,192,256]{2,1,0:T(8,128)(2,1)} %bitcast.120), calls=%async_computation | async-start | bytes 3145728 | tf_op jit(solution)/shard_map/all_to_all | solution.py:54
  160.9 4.2 %fusion.31 = f32[256,512]{1,0:T(8,128)S(1)} fusion(bf16[256,4096]{0,1:T(8,128)(2,1)} %bitcast.118, bf16[4096,512]{1,0:T(8,128)(2,1)} %param.10), kind=kOutput, calls=%fused_computation.64 | convolution fusion | flops 1073741824 | bytes 6815744 | tf_op jit(solution)/shard_map/dot_general | solution.py:59
  165.5 1.4 fusion.9
  166.9 31.5 %psum.7 = f32[256]{0:T(256)S(1)} all-reduce(f32[256]{0:T(256)S(1)} %fusion.9), channel_id=1, replica_groups=mesh['z'=8,'core'=2,'mp'=16] {'mp'}, use_global_device_ids=true, to_apply=%region_2.3 | all-reduce | flops 256 | bytes 2048 | tf_op jit(solution)/shard_map/psum | solution.py:62
  199.0 2.5 fusion.1
  202.2 13.8 %all-to-all-start.4 = ((bf16[16,1,192]{2,1,0:T(2,128)(2,1)}), bf16[16,1,192]{2,1,0:T(2,128)(2,1)S(1)}, u32[]{:S(2)}, u32[]{:S(2)}) async-start(bf16[16,1,192]{2,1,0:T(2,128)(2,1)} %all_to_all.24), calls=%async_computation.4 | async-start | bytes 32768 | tf_op jit(solution)/shard_map/all_to_all | solution.py:71
  216.2 7.1 %all-to-all-done.4 = bf16[16,1,192]{2,1,0:T(2,128)(2,1)S(1)} async-done(((bf16[16,1,192]{2,1,0:T(2,128)(2,1)}), bf16[16,1,192]{2,1,0:T(2,128)(2,1)S(1)}, u32[]{:S(2)}, u32[]{:S(2)}) %all-to-all-start.4) | async-done | bytes 6176 | tf_op jit(solution)/shard_map/all_to_all | solution.py:71
  223.3 1.3 broadcast_in_dim.4
  224.7 3.7 all-to-all-start.1
  228.5 24.8 %all-to-all-done.1 = bf16[16,192,256]{2,1,0:T(8,128)(2,1)S(1)} async-done(((bf16[16,192,256]{2,1,0:T(8,128)(2,1)}), bf16[16,192,256]{2,1,0:T(8,128)(2,1)S(1)}, u32[]{:S(2)}, u32[]{:S(2)}) %all-to-all-start.1) | async-done | bytes 1572896 | tf_op jit(solution)/shard_map/all_to_all | solution.py:19
  253.5 4.9 %fusion.32 = f32[192,896]{1,0:T(8,128)S(1)} fusion(bf16[192,4096]{1,0:T(8,128)(2,1)S(1)} %bitcast.96, bf16[4096,896]{1,0:T(8,128)(2,1)} %bitcast.124), kind=kOutput, calls=%fused_computation.65 | convolution fusion | flops 1409286144 | bytes 9601024 | tf_op jit(solution)/shard_map/dot_general | solution.py:73
  258.5 6.0 %multiply_convert_fusion = (bf16[192,896]{1,0:T(8,128)(2,1)}, bf16[192,896]{1,0:T(8,128)(2,1)}, bf16[192,896]{1,0:T(8,128)(2,1)}) fusion(f32[192,896]{1,0:T(8,128)S(1)} %fusion.32, f32[192]{0:T(256)S(1)} %convert_reduce_fusion, bf16[192,896]{1,0:T(8,128)(2,1)S(1)} %copy-done.6, bf16[192,4096]{1,0:T(8,128)(2,1)S(1)} %bitcast.97, bf16[4096,896]{1,0:T(8,128)(2,1)} %bitcast.125), kind=kOutput, calls=%fused_computation.13 | convolution fusion | flops 1412382720 | bytes 10978048 | tf_op jit(solution)/shard_map/dot_general | solution.py:74
  265.2 32.7 %all-gather.29.cloned.1.call-done = bf16[1536,896]{1,0:T(8,128)(2,1)} async-done(((bf16[192,896]{1,0:T(8,128)(2,1)}), bf16[1536,896]{1,0:T(8,128)(2,1)}) %all-gather.29.cloned.1.call-update) | async-done | bytes 2752528 | tf_op jit(solution)/shard_map/all_gather | solution.py:33
  298.1 43.4 %all-gather.25.cloned.1.call-done = bf16[1536,896]{1,0:T(8,128)(2,1)} async-done(((bf16[192,896]{1,0:T(8,128)(2,1)}), bf16[1536,896]{1,0:T(8,128)(2,1)}) %all-gather.25.cloned.1.call-update) | async-done | bytes 2752528 | tf_op jit(solution)/shard_map/all_gather | solution.py:33
  341.7 47.2 %all_to_all.30 = bf16[16,192,256]{2,1,0:T(8,128)(2,1)S(1)} all-to-all(bf16[16,192,256]{2,1,0:T(8,128)(2,1)S(1)} %fusion.10), channel_id=1, replica_groups=mesh['z'=8,'core'=2,'mp'=16] {'z','core'}, dimensions={0} | all-to-all | bytes 3145728 | tf_op jit(solution)/shard_map/all_to_all | solution.py:7
  388.9 5.2 %convolution_convert_fusion.1 = bf16[256,896]{1,0:T(8,128)(2,1)} fusion(bf16[3072,256]{1,0:T(8,128)(2,1)S(1)} %bitcast.121, bf16[3072,896]{1,0:T(8,128)(2,1)} %bitcast.126), kind=kOutput, calls=%fused_computation.8 | convolution fusion | flops 1409515520 | bytes 7536640 | tf_op jit(solution)/shard_map/dot_general | solution.py:85
  394.1 5.2 %convolution_convert_fusion.2 = bf16[256,896]{1,0:T(8,128)(2,1)} fusion(bf16[3072,256]{1,0:T(8,128)(2,1)S(1)} %bitcast.122, bf16[3072,896]{1,0:T(8,128)(2,1)} %bitcast.127), kind=kOutput, calls=%fused_computation.9 | convolution fusion | flops 1409515520 | bytes 7536640 | tf_op jit(solution)/shard_map/dot_general | solution.py:82
  (64 shorter events, 5.9 us)
Async XLA Ops:
  7.2 56.1 %all-gather.21.cloned.1.call-start = ((), (), s32[]{:S(2)}) async-start(), calls=%async_computation.7 | async-start | bytes 4128768 | tf_op jit(solution)/shard_map/all_gather | solution.py:33
  7.9 105.6 %all-gather.17.cloned.1.call-start = ((), (), s32[]{:S(2)}) async-start(), calls=%async_computation.5 | async-start | bytes 4128768 | tf_op jit(solution)/shard_map/all_gather | solution.py:33
  8.6 244.8 %all-gather.23.cloned.1.call-start = ((), (), s32[]{:S(2)}) async-start(), calls=%async_computation.8 | async-start | bytes 11010048 | tf_op jit(solution)/shard_map/all_gather | solution.py:34
  63.3 195.2 %all-gather.19.cloned.1.call-start = ((), (), s32[]{:S(2)}) async-start(), calls=%async_computation.6 | async-start | bytes 11010048 | tf_op jit(solution)/shard_map/all_gather | solution.py:34
  113.5 0.9 copy-start.2
  116.0 6.7 %copy-start.3 = (s32[16,192]{1,0:T(8,128)S(1)}, s32[16,192]{1,0:T(8,128)}, u32[]{:S(2)}) copy-start(s32[16,192]{1,0:T(8,128)} %param.13) | copy-start | bytes 36868
  116.0 6.7 %copy-start.4 = (s32[16]{0:T(128)S(1)}, s32[16]{0:T(128)}, u32[]{:S(2)}) copy-start(s32[16]{0:T(128)} %param.14) | copy-start | bytes 196
  116.0 36.9 %all-to-all-start.3 = ((bf16[16,256,256]{1,2,0:T(8,128)(2,1)}), bf16[16,256,256]{1,2,0:T(8,128)(2,1)S(1)}, u32[]{:S(2)}, u32[]{:S(2)}) async-start(bf16[16,256,256]{1,2,0:T(8,128)(2,1)} %broadcast_in_dim.5), calls=%async_computation.3 | async-start | bytes 4194304 | tf_op jit(solution)/shard_map/all_to_all | solution.py:19
  152.9 1.3 copy-start
  154.3 47.9 %all-to-all-start = ((bf16[16,192,256]{2,1,0:T(8,128)(2,1)}), bf16[16,192,256]{2,1,0:T(8,128)(2,1)S(1)}, u32[]{:S(2)}, u32[]{:S(2)}) async-start(bf16[16,192,256]{2,1,0:T(8,128)(2,1)} %bitcast.120), calls=%async_computation | async-start | bytes 3145728 | tf_op jit(solution)/shard_map/all_to_all | solution.py:54
  160.8 4.3 %copy-start.1 = (bf16[16,256,256]{1,2,0:T(8,128)(2,1)S(1)}, bf16[16,256,256]{1,2,0:T(8,128)(2,1)}, u32[]{:S(2)}) copy-start(bf16[16,256,256]{1,2,0:T(8,128)(2,1)} %copy-done) | copy-start | bytes 6291460
  160.8 4.7 %copy-start.5 = (bf16[4096,512]{1,0:T(8,128)(2,1)S(1)}, bf16[4096,512]{1,0:T(8,128)(2,1)}, u32[]{:S(2)}) copy-start(bf16[4096,512]{1,0:T(8,128)(2,1)} %param.11) | copy-start | bytes 12582916
  160.8 4.7 %copy-start.7 = (f32[512]{0:T(512)S(1)}, f32[512]{0:T(512)}, u32[]{:S(2)}) copy-start(f32[512]{0:T(512)} %param.12) | copy-start | bytes 6148
  202.2 21.2 %all-to-all-start.4 = ((bf16[16,1,192]{2,1,0:T(2,128)(2,1)}), bf16[16,1,192]{2,1,0:T(2,128)(2,1)S(1)}, u32[]{:S(2)}, u32[]{:S(2)}) async-start(bf16[16,1,192]{2,1,0:T(2,128)(2,1)} %all_to_all.24), calls=%async_computation.4 | async-start | bytes 32768 | tf_op jit(solution)/shard_map/all_to_all | solution.py:71
  224.7 28.6 %all-to-all-start.1 = ((bf16[16,192,256]{2,1,0:T(8,128)(2,1)}), bf16[16,192,256]{2,1,0:T(8,128)(2,1)S(1)}, u32[]{:S(2)}, u32[]{:S(2)}) async-start(bf16[16,192,256]{2,1,0:T(8,128)(2,1)} %broadcast_in_dim.4), calls=%async_computation.1 | async-start | bytes 3145728 | tf_op jit(solution)/shard_map/all_to_all | solution.py:19
  228.4 69.5 %all-gather.29.cloned.1.call-start = ((), (), s32[]{:S(2)}) async-start(), calls=%async_computation.11 | async-start | bytes 3096576 | tf_op jit(solution)/shard_map/all_gather | solution.py:33
  253.5 5.0 %copy-start.6 = (bf16[192,896]{1,0:T(8,128)(2,1)S(1)}, bf16[192,896]{1,0:T(8,128)(2,1)}, u32[]{:S(2)}) copy-start(bf16[192,896]{1,0:T(8,128)(2,1)} %param.17) | copy-start | bytes 1032196
  264.5 76.9 %all-gather.25.cloned.1.call-start = ((), (), s32[]{:S(2)}) async-start(), calls=%async_computation.9 | async-start | bytes 3096576 | tf_op jit(solution)/shard_map/all_gather | solution.py:33
  265.1 123.8 %all-gather.31.cloned.1.call-start = ((), (), s32[]{:S(2)}) async-start(), calls=%async_computation.12 | async-start | bytes 8257536 | tf_op jit(solution)/shard_map/all_gather | solution.py:34
  297.9 96.2 %all-gather.27.cloned.1.call-start = ((), (), s32[]{:S(2)}) async-start(), calls=%async_computation.10 | async-start | bytes 8257536 | tf_op jit(solution)/shard_map/all_gather | solution.py:34
Sparse Core Ops, SparseCore 0:
  9.8 53.4 all-gather.20
  65.0 48.4 all-gather.16
  115.3 23.1 all-gather.22
  140.1 25.0 all-gather.18
  264.7 33.1 all-gather.28
  300.1 41.3 all-gather.24
  343.3 23.0 all-gather.30
  368.1 22.2 all-gather.26
